TPU v7x, 512 devices: a whole 4x8x8 slice. The times are simulated.
512 devices in a mesh: wide: 128 (over y, z, core), pair: 4 (over x).
Axes of the slice: x: 4, y: 8, z: 8, core: 2. Of those that a mesh axis runs over, the one named last changes fastest.
Arguments:
- blocks: bfloat16 [2048, 1024, 512], P('pair', 'wide'), may hold values from -6 to 6
- basis_a: bfloat16 [1024, 64], replicated, may hold values from -0.1875 to 0.1875
- basis_b: bfloat16 [512, 64], replicated, may hold values from -0.25 to 0.25
- sketch: bfloat16 [2048, 64], P(('pair', 'wide')), may hold values from -6 to 6
Outputs:
- transfer: float32 [4096, 64], P(('wide', 'pair'))
- coefficients: float32 [2048, 64], P(('pair', 'wide'))
All inputs are finite; a program needn't handle non-finite values.
Results may differ from a plain program's by a relative error of at most 0.0041.
Values may be sent and summed in bfloat16 or wider, within the bound.
A program may use at most 64 MiB of HBM per device.

v0:
```python
import jax
import jax.numpy as jnp
from jax import lax
from jax.sharding import PartitionSpec as P


def orthonormal(sketched, gram):
    lower = jnp.linalg.cholesky(gram)
    return lax.linalg.triangular_solve(
        lower, sketched, left_side=False, lower=True, transpose_a=True
    )


def per_device(blocks, basis_a, basis_b, sketch):
    fibres = sketch.shape[0]
    rank_a = basis_a.shape[1]
    rank_b = basis_b.shape[1]
    narrowed = jnp.einsum(
        "fac,cr->far", blocks, basis_b, preferred_element_type=jnp.float32
    ).astype(jnp.bfloat16)
    regrouped = lax.all_to_all(narrowed, "wide", split_axis=0, concat_axis=1, tiled=True)
    projected = jnp.einsum(
        "ap,far->fpr", basis_a, regrouped, preferred_element_type=jnp.float32
    ).astype(jnp.bfloat16)
    projected = projected.reshape(fibres, rank_a * rank_b)
    partial_value = jnp.einsum("fj,fk->jk", projected, sketch, preferred_element_type=jnp.float32)
    own_count = rank_a * rank_b // lax.axis_size(("wide", "pair"))
    sketch_all = lax.psum(partial_value, ("wide", "pair"))
    gram_matrix = jnp.dot(sketch_all.T, sketch_all, precision=lax.Precision.HIGHEST)
    parent_basis = orthonormal(sketch_all, gram_matrix)
    first_row = lax.axis_index(("wide", "pair")) * own_count
    own_basis = lax.dynamic_slice_in_dim(parent_basis, first_row, own_count, 0)
    transfer = own_basis * jnp.sqrt(jnp.float32(rank_a * rank_b))
    coefficients = jnp.dot(
        projected.astype(jnp.float32), parent_basis, precision=lax.Precision.HIGHEST
    )
    return (transfer, coefficients)


def solution(mesh):
    placed = (P("pair", "wide", None), P(), P(), P(("pair", "wide"), None))
    return jax.shard_map(
        per_device,
        mesh=mesh,
        in_specs=placed,
        out_specs=(P(("wide", "pair"), None), P(("pair", "wide"), None)),
        check_vma=False,
    )
```

profile of v0, /device:TPU:24, one launch (start us, length us, event | category | flops | bytes accessed | tf_op | source)
XLA Modules:
  0.0 346.8 jit_solution(4763148819996868437)
XLA Ops:
  7.2 0.0 copy-start
  7.2 0.0 all-reduce.2.cloned.1.call-start
  7.2 3.4 convolution_convert_fusion
  10.7 0.0 copy-start.1
  10.7 0.6 reshape.19
  11.3 35.6 %all_to_all.18 = bf16[128,2,1024]{2,1,0:T(2,128)(2,1)S(1)} all-to-all(bf16[128,2,1024]{2,1,0:T(2,128)(2,1)S(1)} %reshape.19), channel_id=1, replica_groups=mesh['wide'=128,'pair'=4] {'wide'}, dimensions={0} | all-to-all | bytes 1048576 | tf_op jit(solution)/shard_map/all_to_all | solution.py:21
  46.9 0.6 reshape.20
  47.5 0.0 copy-done
  47.5 0.5 fusion
  48.0 0.1 copy.19
  48.1 0.1 reshape.16
  48.2 0.0 copy-done.1
  48.2 1.4 fusion.9
  49.6 0.0 all-reduce.2.cloned.1.call-update
  49.6 271.4 %all-reduce.2.cloned.1.call-done = f32[4096,64]{0,1:T(8,128)} async-done(((f32[4096,64]{0,1:T(8,128)}), f32[4096,64]{0,1:T(8,128)}) %all-reduce.2.cloned.1.call-update) | async-done | bytes 1048592 | tf_op jit(solution)/shard_map/psum | solution.py:28
  321.0 2.5 fusion.10
  323.5 0.1 copy.20
  323.6 5.8 %cholesky.16 = f32[64,64]{1,0:T(8,128)S(1)} custom-call(f32[64,64]{1,0:T(8,128)S(1)} %fusion.8), custom_call_target="Cholesky" | custom-call | tf_op jit(solution)/shard_map/jit(cholesky)/cholesky | solution.py:8
  329.5 0.6 compare_reduce_fusion
  330.2 0.7 fusion.5
  330.8 4.9 %custom-call.6 = f32[1,64,64]{1,2,0:T(8,128)S(1)} custom-call(f32[1,64,64]{2,1,0:T(8,128)S(1)} %fusion.5), custom_call_target="InvertDiagBlocksLowerTriangular" | custom-call | tf_op jit(solution)/shard_map/triangular_solve | solution.py:9
  335.7 2.3 fusion.6
  338.0 1.2 fusion.11
  339.2 0.1 dynamic-slice_multiply_fusion
  339.3 0.7 copy.21
  (2 shorter events, 0.0 us)
Async XLA Ops:
  7.2 40.3 %copy-start = (bf16[1024,64]{0,1:T(8,128)(2,1)S(1)}, bf16[1024,64]{0,1:T(8,128)(2,1)}, u32[]{:S(2)}) copy-start(bf16[1024,64]{0,1:T(8,128)(2,1)} %param.5) | copy-start | bytes 393220
  7.2 313.8 %all-reduce.2.cloned.1.call-start = ((), (), s32[]{:S(2)}) async-start(), calls=%async_computation.1 | async-start | bytes 2097152 | tf_op jit(solution)/shard_map/psum | solution.py:28
  10.7 37.5 %copy-start.1 = (bf16[4,64]{1,0:T(4,128)(2,1)S(1)}, bf16[4,64]{1,0:T(4,128)(2,1)}, u32[]{:S(2)}) copy-start(bf16[4,64]{1,0:T(4,128)(2,1)} %param.7) | copy-start | bytes 1540
Sparse Core Ops, SparseCore 0:
  49.7 271.2 all-reduce.1
where the time goes:
time: 347 us
  waiting for transfers between devices  271 us (78%)
  blocking collectives  35.6 us (10%)
  between operations  14.1 us (4%)
  other arithmetic  12.2 us (4%)
  matrix products  11.3 us (3%)
    psum x1, waiting for transfers between devices, per_device(): sketch_all = lax.psum(partial_value, ('wide', 'pair'))  271 us
    all_to_all x1, blocking collectives, per_device(): lax.all_to_all(narrowed, 'wide', split_axis=0, concat_axis=1, tiled=True)  35.6 us
  transfers between devices with their start and end apart: 1, of which 1 were waited for; matrix products, arithmetic and copies ran while one was open for 0% of the time, Pallas kernels for 0%

commit v1 on v0

--- a/solution.py
+++ b/solution.py
@@ -2,6 +2,7 @@
 import jax.numpy as jnp
 from jax import lax
 from jax.sharding import PartitionSpec as P
+from jax.lax import psum
 
 
 def orthonormal(sketched, gram):
@@ -25,7 +26,9 @@
     projected = projected.reshape(fibres, rank_a * rank_b)
     partial_value = jnp.einsum("fj,fk->jk", projected, sketch, preferred_element_type=jnp.float32)
     own_count = rank_a * rank_b // lax.axis_size(("wide", "pair"))
-    sketch_all = lax.psum(partial_value, ("wide", "pair"))
+    sketch_all = partial_value
+    for hop_no in ("wide", "pair"):
+        sketch_all = psum(sketch_all, hop_no)
     gram_matrix = jnp.dot(sketch_all.T, sketch_all, precision=lax.Precision.HIGHEST)
     parent_basis = orthonormal(sketch_all, gram_matrix)
     first_row = lax.axis_index(("wide", "pair")) * own_count

time: 347 us -> 325 us (0.937)
  the two profiles are of different devices: /device:TPU:24 before, /device:TPU:8 now
where the time goes in v1:
time: 325 us; the launch traced here: 324 us
  waiting for transfers between devices  247 us (76%)
  blocking collectives  37.5 us (12%)
  between operations  14.2 us (4%)
  other arithmetic  12.2 us (4%)
  matrix products  11.4 us (4%)
    psum x2, waiting for transfers between devices, per_device(): sketch_all = psum(sketch_all, hop_no)  247 us
    all_to_all x1, blocking collectives, per_device(): lax.all_to_all(narrowed, 'wide', split_axis=0, concat_axis=1, tiled=True)  37.5 us
    another operation x3, other arithmetic, orthonormal(): lower = jnp.linalg.cholesky(gram)  6.52 us
  transfers between devices with their start and end apart: 2, of which 2 were waited for; matrix products, arithmetic and copies ran while one was open for 0% of the time, Pallas kernels for 0%

profile of v1, /device:TPU:8, one launch (start us, length us, event | category | flops | bytes accessed | tf_op | source)
XLA Modules:
  0.0 324.4 jit_solution(1043105510741689203)
XLA Ops:
  7.2 0.0 copy-start
  7.2 0.0 all-reduce.3.cloned.1.call-start
  7.2 3.4 %convolution_convert_fusion = bf16[512,8,64]{2,1,0:T(8,128)(2,1)S(1)} fusion(bf16[512,8,512]{2,1,0:T(8,128)(2,1)} %param.4, bf16[512,64]{0,1:T(8,128)(2,1)} %param.6), kind=kOutput, calls=%fused_computation | convolution fusion | flops 268697600 | bytes 4784128 | tf_op jit(solution)/shard_map/fac,cr->far/dot_general | solution.py:19
  10.7 0.0 copy-start.1
  10.7 0.6 reshape.19
  11.3 37.5 %all_to_all.18 = bf16[128,2,1024]{2,1,0:T(2,128)(2,1)S(1)} all-to-all(bf16[128,2,1024]{2,1,0:T(2,128)(2,1)S(1)} %reshape.19), channel_id=1, replica_groups=mesh['wide'=128,'pair'=4] {'wide'}, dimensions={0} | all-to-all | bytes 1048576 | tf_op jit(solution)/shard_map/all_to_all | solution.py:22
  48.7 0.6 reshape.20
  49.3 0.0 copy-done
  49.4 0.5 fusion
  49.9 0.1 copy.19
  50.0 0.1 reshape.16
  50.1 0.0 copy-done.1
  50.1 1.4 fusion.9
  51.5 0.0 all-reduce.3.cloned.1.call-update
  51.5 0.0 all-reduce.5.cloned.1.call-start
  51.5 190.0 %all-reduce.3.cloned.1.call-done = f32[4096,64]{0,1:T(8,128)} async-done(((f32[4096,64]{0,1:T(8,128)}), f32[4096,64]{0,1:T(8,128)}) %all-reduce.3.cloned.1.call-update) | async-done | bytes 1048592 | tf_op jit(solution)/shard_map/psum | solution.py:31
  241.5 0.0 all-reduce.5.cloned.1.call-update
  241.6 57.0 %all-reduce.5.cloned.1.call-done = f32[4096,64]{0,1:T(8,128)} async-done(((f32[4096,64]{0,1:T(8,128)}), f32[4096,64]{0,1:T(8,128)}) %all-reduce.5.cloned.1.call-update) | async-done | bytes 1048592 | tf_op jit(solution)/shard_map/psum | solution.py:31
  298.5 2.6 fusion.10
  301.2 0.1 copy.20
  301.3 5.8 %cholesky.16 = f32[64,64]{1,0:T(8,128)S(1)} custom-call(f32[64,64]{1,0:T(8,128)S(1)} %fusion.8), custom_call_target="Cholesky" | custom-call | tf_op jit(solution)/shard_map/jit(cholesky)/cholesky | solution.py:9
  307.2 0.6 compare_reduce_fusion
  307.8 0.7 fusion.5
  308.5 4.9 %custom-call.6 = f32[1,64,64]{1,2,0:T(8,128)S(1)} custom-call(f32[1,64,64]{2,1,0:T(8,128)S(1)} %fusion.5), custom_call_target="InvertDiagBlocksLowerTriangular" | custom-call | tf_op jit(solution)/shard_map/triangular_solve | solution.py:10
  313.4 2.3 fusion.6
  315.6 1.2 fusion.11
  316.8 0.1 dynamic-slice_multiply_fusion
  316.9 0.7 copy.21
  (2 shorter events, 0.0 us)
Async XLA Ops:
  7.2 42.2 %copy-start = (bf16[1024,64]{0,1:T(8,128)(2,1)S(1)}, bf16[1024,64]{0,1:T(8,128)(2,1)}, u32[]{:S(2)}) copy-start(bf16[1024,64]{0,1:T(8,128)(2,1)} %param.5) | copy-start | bytes 393220
  7.2 234.4 %all-reduce.3.cloned.1.call-start = ((), (), s32[]{:S(2)}) async-start(), calls=%async_computation.1 | async-start | bytes 2097152 | tf_op jit(solution)/shard_map/psum | solution.py:31
  10.7 39.4 %copy-start.1 = (bf16[4,64]{1,0:T(4,128)(2,1)S(1)}, bf16[4,64]{1,0:T(4,128)(2,1)}, u32[]{:S(2)}) copy-start(bf16[4,64]{1,0:T(4,128)(2,1)} %param.7) | copy-start | bytes 1540
  51.5 247.0 %all-reduce.5.cloned.1.call-start = ((), (), s32[]{:S(2)}) async-start(), calls=%async_computation.2 | async-start | bytes 2097152 | tf_op jit(solution)/shard_map/psum | solution.py:31
Sparse Core Ops, SparseCore 0:
  51.6 189.8 all-reduce.2
  243.9 54.5 all-reduce.4
